TPU v7x, 256 devices: a whole 4x4x8 slice. The times are simulated.
256 devices in a mesh: ctx: 16 (over y_hi, x, core), dp: 16 (over y_lo, z).
Axes of the slice: x: 4, y: 4 (y_hi: 2, y_lo: 2; y = y_hi * 2 + y_lo), z: 8, core: 2. Of those that a mesh axis runs over, the one named last changes fastest.
Arguments:
- queries: bfloat16 [16, 2048, 1536], P('dp', 'ctx'), as said below
- keys: bfloat16 [16, 2048, 1536], P('dp', 'ctx'), as said below
- values: bfloat16 [16, 2048, 1536], P('dp', 'ctx'), may hold values from -6 to 6
- tangent_queries: bfloat16 [16, 2048, 1536], P('dp', 'ctx'), may hold values from -6 to 6
- tangent_keys: bfloat16 [16, 2048, 1536], P('dp', 'ctx'), may hold values from -6 to 6
- tangent_values: bfloat16 [16, 2048, 1536], P('dp', 'ctx'), may hold values from -6 to 6
- clip_ids: int32 [16, 2048], P('dp', 'ctx'), may hold values from 0 to 3, never falling along the last dimension, each value on 1 to 1024 neighbouring positions
- block_order: int32 [16], replicated, may hold values from 0 to 15, each once
- out_weight: bfloat16 [1536, 3072], replicated, may hold values from -0.15625 to 0.15625
- layer_scale: float32 [3072], replicated, may hold values from 0.1 to 1.9
- cotangent: bfloat16 [16, 2048, 3072], P('dp', 'ctx'), as said below
Outputs:
- tangent_branch: bfloat16 [16, 2048, 3072], P('dp', 'ctx')
- scale_grad: float32 [3072], replicated
Inputs may be any that keep to these rules, and one draw needn't show every extreme that they name: `clip_ids`: ids never fall along a sample's rows; each of the 4 clips is a run of consecutive rows. `block_order`: each block number appears once. `queries`: real-valued. `keys`: real-valued. `cotangent`: real-valued.
All inputs are finite; a program needn't handle non-finite values.
Results may differ from a plain program's by a relative error of at most 0.02.
The roundings to bfloat16 on the way count: a program that leaves them out, or rounds other values in their place, can miss the bound.
Values may be sent and summed in bfloat16 or wider, within the bound.
A program may use at most 192 MiB of HBM per device.

v0:
```python
import math
import jax
import jax.numpy as jnp
from jax import lax
from jax.sharding import PartitionSpec as P

HEADS = 12


def rotate(x, pos, half_dim):
    frequency = 10000.0 ** (-jnp.arange(half_dim, dtype=jnp.float32) / half_dim)
    angles = pos.astype(jnp.float32)[:, None] * frequency[None, :]
    cosine = jnp.cos(angles)[:, None, :]
    sine_part = jnp.sin(angles)[:, None, :]
    front_part = x[..., :half_dim]
    back_part = x[..., half_dim:]
    return jnp.concatenate(
        [front_part * cosine - back_part * sine_part, back_part * cosine + front_part * sine_part],
        axis=-1,
    )


def make_attend(query_rot, tquery_rot, query_ids, scale):

    def attend(carry, block):
        best, total, weighted, primal_acc, slope_acc, spread_acc = carry
        key_blk, value_blk, tkey_blk, tvalue_blk, key_ids = block
        scores = (
            jnp.einsum("hqd,hkd->hqk", query_rot, key_blk, preferred_element_type=jnp.float32)
            * scale
        )
        same_clip = query_ids[:, None] == key_ids[None, :]
        scores = jnp.where(same_clip[None], scores, -jnp.inf)
        slopes = (
            jnp.einsum("hqd,hkd->hqk", tquery_rot, key_blk, preferred_element_type=jnp.float32)
            + jnp.einsum("hqd,hkd->hqk", query_rot, tkey_blk, preferred_element_type=jnp.float32)
        ) * scale
        new_best = jnp.maximum(best, jnp.max(scores, axis=-1))
        factor = jnp.exp(best - new_best)
        weights = jnp.exp(scores - new_best[..., None])
        tilted = weights * slopes
        total = total * factor + jnp.sum(weights, axis=-1)
        weighted = weighted * factor + jnp.sum(tilted, axis=-1)
        weights_b = weights.astype(jnp.bfloat16)
        tilted_b = tilted.astype(jnp.bfloat16)
        primal_acc = primal_acc * factor[..., None] + jnp.einsum(
            "hqk,hkd->hqd", weights_b, value_blk, preferred_element_type=jnp.float32
        )
        slope_acc = slope_acc * factor[..., None] + jnp.einsum(
            "hqk,hkd->hqd", tilted_b, value_blk, preferred_element_type=jnp.float32
        )
        spread_acc = spread_acc * factor[..., None] + jnp.einsum(
            "hqk,hkd->hqd", weights_b, tvalue_blk, preferred_element_type=jnp.float32
        )
        return ((new_best, total, weighted, primal_acc, slope_acc, spread_acc), None)

    return attend


def start_states(heads, rows, head_dim):
    zeros_rows = jnp.zeros((heads, rows), jnp.float32)
    zeros_heads = jnp.zeros((heads, rows, head_dim), jnp.float32)
    return (
        jnp.full((heads, rows), -1e30, jnp.float32),
        zeros_rows,
        zeros_rows,
        zeros_heads,
        zeros_heads,
        zeros_heads,
    )


def local(
    queries,
    keys,
    values,
    tangent_queries,
    tangent_keys,
    tangent_values,
    clip_ids,
    block_order,
    out_weight,
    layer_scale,
    cotangent,
):
    tok_rows = queries.shape[1]
    heads = HEADS
    head_dim = queries.shape[2] // heads
    scale = head_dim ** (-0.5)
    cycle_index = lax.axis_index("ctx")
    positions = block_order[cycle_index] * tok_rows + jnp.arange(tok_rows, dtype=jnp.int32)

    def heads_first(x, turned):
        y = x[0].reshape(tok_rows, heads, head_dim)
        if turned:
            y = rotate(y.astype(jnp.float32), positions, head_dim // 2).astype(jnp.bfloat16)
        return jnp.transpose(y, (1, 0, 2))

    query_rot = heads_first(queries, True)
    key_rot = heads_first(keys, True)
    value_heads = heads_first(values, False)
    tquery_rot = heads_first(tangent_queries, True)
    tkey_rot = heads_first(tangent_keys, True)
    tvalue_heads = heads_first(tangent_values, False)
    all_ids = lax.all_gather(clip_ids, "ctx", axis=1, tiled=True)[0]
    own_ids = clip_ids[0]
    attend = make_attend(query_rot, tquery_rot, own_ids, scale)
    carry = start_states(heads, tok_rows, head_dim)
    key_part = lax.all_gather(key_rot, "ctx", axis=1, tiled=True)
    value_part = lax.all_gather(value_heads, "ctx", axis=1, tiled=True)
    tkey_part = lax.all_gather(tkey_rot, "ctx", axis=1, tiled=True)
    tvalue_part = lax.all_gather(tvalue_heads, "ctx", axis=1, tiled=True)
    count = key_part.shape[1]
    block_rows = math.gcd(count, tok_rows)
    blocks = count // block_rows

    def split_blocks(x):
        return jnp.transpose(x.reshape(heads, blocks, block_rows, head_dim), (1, 0, 2, 3))

    stacked = (
        split_blocks(key_part),
        split_blocks(value_part),
        split_blocks(tkey_part),
        split_blocks(tvalue_part),
        all_ids.reshape(blocks, block_rows),
    )
    carry, unused = lax.scan(attend, carry, stacked)
    best, total, weighted, primal_acc, slope_acc, spread_acc = carry
    mean_out = primal_acc / total[..., None]
    tangent_heads = (
        (slope_acc + spread_acc) / total[..., None] - (weighted / total)[..., None] * mean_out
    ).astype(jnp.bfloat16)
    tangent_rows = jnp.transpose(tangent_heads, (1, 0, 2)).reshape(tok_rows, heads * head_dim)
    projected = jnp.dot(tangent_rows, out_weight, preferred_element_type=jnp.float32)
    branch = (layer_scale * projected).astype(jnp.bfloat16)[None]
    partial_grad = jnp.sum(cotangent[0].astype(jnp.float32) * projected, axis=0)
    summed = lax.psum(partial_grad, ("ctx", "dp"))
    count_all = lax.axis_size("ctx") * lax.axis_size("dp") * tok_rows
    return (branch, summed / math.sqrt(count_all))


def solution(mesh):
    in_specs = (
        P("dp", "ctx", None),
        P("dp", "ctx", None),
        P("dp", "ctx", None),
        P("dp", "ctx", None),
        P("dp", "ctx", None),
        P("dp", "ctx", None),
        P("dp", "ctx"),
        P(),
        P(),
        P(),
        P("dp", "ctx", None),
    )
    out_specs = (P("dp", "ctx", None), P())
    return jax.shard_map(local, mesh=mesh, in_specs=in_specs, out_specs=out_specs, check_vma=False)
```

profile of v0, /device:TPU:1, one launch (start us, length us, event | category | flops | bytes accessed | tf_op | source)
XLA Modules:
  0.0 623.5 jit_solution(16415383374081786712)
XLA Ops:
  18.6 1.9 copy.28
  22.8 25.8 %all_gather.15 = s32[1,2048]{1,0:T(1,128)} all-gather(s32[1,128]{1,0:T(1,128)} %param.19), channel_id=1, replica_groups=mesh['ctx'=16,'dp'=16] {'ctx'}, dimensions={1}, use_global_device_ids=true | all-gather | bytes 8704 | tf_op jit(solution)/shard_map/all_gather | solution.py:105
  48.7 46.9 %all-gather.5.cloned.1.call-done = bf16[12,2048,128]{1,2,0:T(8,128)(2,1)} async-done(((bf16[12,128,128]{1,2,0:T(8,128)(2,1)}), bf16[12,2048,128]{1,2,0:T(8,128)(2,1)}) %all-gather.5.cloned.1.call-update) | async-done | bytes 6291472 | tf_op jit(solution)/shard_map/all_gather | solution.py:109
  95.6 7.8 %copy.44 = bf16[192,8,16,128]{3,2,1,0:T(8,128)(2,1)} copy(bf16[192,8,16,128]{3,1,2,0:T(8,128)(2,1)} %bitcast.120) | data formatting | bytes 12582912
  103.3 9.0 %copy.21 = bf16[12,16,128,128]{3,2,0,1:T(8,128)(2,1)} copy(bf16[12,16,128,128]{2,1,3,0:T(8,128)(2,1)} %bitcast.115) | data formatting | bytes 12582912 | tf_op jit(solution)/shard_map/reshape | solution.py:118
  112.4 58.9 %all-gather.7.cloned.1.call-done = bf16[12,2048,128]{1,2,0:T(8,128)(2,1)} async-done(((bf16[12,128,128]{1,2,0:T(8,128)(2,1)}), bf16[12,2048,128]{1,2,0:T(8,128)(2,1)}) %all-gather.7.cloned.1.call-update) | async-done | bytes 6291472 | tf_op jit(solution)/shard_map/all_gather | solution.py:111
  171.3 8.7 %copy.25 = bf16[12,2048,128]{2,1,0:T(8,128)(2,1)} copy(bf16[12,2048,128]{1,2,0:T(8,128)(2,1)} %all-gather.7.cloned.1.call-done) | data formatting | bytes 12582912 | tf_op jit(solution)/shard_map/all_gather | solution.py:111
  180.0 67.1 %all-gather.9.cloned.1.call-done = bf16[12,2048,128]{1,2,0:T(8,128)(2,1)} async-done(((bf16[12,128,128]{1,2,0:T(8,128)(2,1)}), bf16[12,2048,128]{1,2,0:T(8,128)(2,1)}) %all-gather.9.cloned.1.call-update) | async-done | bytes 6291472 | tf_op jit(solution)/shard_map/all_gather | solution.py:110
  247.1 8.6 %copy.27 = bf16[12,2048,128]{2,1,0:T(8,128)(2,1)} copy(bf16[12,2048,128]{1,2,0:T(8,128)(2,1)} %all-gather.9.cloned.1.call-done) | data formatting | bytes 12582912 | tf_op jit(solution)/shard_map/all_gather | solution.py:110
  255.7 67.0 %all-gather.11.cloned.1.call-done = bf16[12,2048,128]{1,2,0:T(8,128)(2,1)} async-done(((bf16[12,128,128]{1,2,0:T(8,128)(2,1)}), bf16[12,2048,128]{1,2,0:T(8,128)(2,1)}) %all-gather.11.cloned.1.call-update) | async-done | bytes 6291472 | tf_op jit(solution)/shard_map/all_gather | solution.py:112
  322.7 8.7 %copy.29 = bf16[12,2048,128]{2,1,0:T(8,128)(2,1)} copy(bf16[12,2048,128]{1,2,0:T(8,128)(2,1)} %all-gather.11.cloned.1.call-done) | data formatting | bytes 12582912 | tf_op jit(solution)/shard_map/all_gather | solution.py:112
  331.3 200.5 %while.21 = (s32[]{:T(128)}, f32[12,128]{1,0:T(8,128)S(1)}, f32[12,128]{1,0:T(8,128)}, f32[12,128]{1,0:T(8,128)}, f32[12,128,128]{2,1,0:T(8,128)S(1)}, /*index=5...) while((s32[]{:T(128)}, f32[12,128]{1,0:T(8,128)S(1)}, ...), condition=%wide.region_4.5_spmd.clone, body=%wide.region_0.4_spmd.clone.sunk | while | flops 306735616 | bytes 14789864 | solution.py:127
  337.8 1.6 convolution_add_fusion.9
  339.3 1.6 convolution_add_fusion.8
  340.9 1.6 convolution_add_fusion.7
  350.3 1.6 convolution_add_fusion.9
  351.9 1.6 convolution_add_fusion.8
  353.5 1.6 convolution_add_fusion.7
  362.9 1.6 convolution_add_fusion.9
  364.5 1.6 convolution_add_fusion.8
  366.0 1.6 convolution_add_fusion.7
  375.5 1.6 convolution_add_fusion.9
  377.0 1.6 convolution_add_fusion.8
  378.6 1.6 convolution_add_fusion.7
  388.1 1.6 convolution_add_fusion.9
  389.6 1.6 convolution_add_fusion.8
  391.2 1.6 convolution_add_fusion.7
  400.6 1.6 convolution_add_fusion.9
  402.2 1.6 convolution_add_fusion.8
  403.8 1.6 convolution_add_fusion.7
  413.2 1.6 convolution_add_fusion.9
  414.8 1.6 convolution_add_fusion.8
  416.3 1.6 convolution_add_fusion.7
  425.8 1.6 convolution_add_fusion.9
  427.4 1.6 convolution_add_fusion.8
  428.9 1.6 convolution_add_fusion.7
  438.4 1.6 convolution_add_fusion.9
  439.9 1.6 convolution_add_fusion.8
  441.5 1.6 convolution_add_fusion.7
  450.9 1.6 convolution_add_fusion.9
  452.5 1.6 convolution_add_fusion.8
  454.1 1.6 convolution_add_fusion.7
  463.5 1.6 convolution_add_fusion.9
  465.1 1.6 convolution_add_fusion.8
  466.6 1.6 convolution_add_fusion.7
  476.1 1.6 convolution_add_fusion.9
  477.6 1.6 convolution_add_fusion.8
  479.2 1.6 convolution_add_fusion.7
  484.4 1.5 fusion.72
  488.6 1.6 convolution_add_fusion.9
  490.2 1.6 convolution_add_fusion.8
  491.8 1.6 convolution_add_fusion.7
  501.2 1.6 convolution_add_fusion.9
  502.8 1.6 convolution_add_fusion.8
  504.3 1.6 convolution_add_fusion.7
  513.8 1.6 convolution_add_fusion.9
  515.3 1.6 convolution_add_fusion.8
  516.9 1.6 convolution_add_fusion.7
  522.1 1.5 fusion.72
  526.4 1.6 convolution_add_fusion.9
  527.9 1.6 convolution_add_fusion.8
  529.5 1.6 convolution_add_fusion.7
  534.3 6.4 %fusion.32 = (f32[3072]{0:T(1024)S(1)}, bf16[1,128,3072]{2,1,0:T(8,128)(2,1)}) fusion(bf16[1,128,3072]{2,1,0:T(8,128)(2,1)} %param.23, f32[3072]{0:T(1024)S(1)} %copy-done.3, bf16[128,1536]{0,1:T(8,128)(2,1)S(1)} %bitcast.121, bf16[1536,3072]{1,0:T(8,128)(2,1)} %param.21), kind=kOutput, calls=%fused_computation.46 | convolution fusion | flops 1209922560 | bytes 11427840 | tf_op jit(solution)/shard_map/dot_general | solution.py:134
  540.7 75.7 %psum.7 = f32[3072]{0:T(1024)S(1)} all-reduce(f32[3072]{0:T(1024)S(1)} %get-tuple-element.187), channel_id=1, replica_groups=mesh['ctx'=16,'dp'=16] {'ctx','dp'}, use_global_device_ids=true, to_apply=%region_6.7 | all-reduce | flops 3072 | bytes 24576 | tf_op jit(solution)/shard_map/psum | solution.py:137
  (265 shorter events, 136.7 us)
Async XLA Ops:
  7.2 88.4 %all-gather.5.cloned.1.call-start = ((), (), s32[]{:S(2)}) async-start(), calls=%async_computation | async-start | bytes 6684672 | tf_op jit(solution)/shard_map/all_gather | solution.py:109
  11.7 5.9 copy-start.2
  16.6 154.7 %all-gather.7.cloned.1.call-start = ((), (), s32[]{:S(2)}) async-start(), calls=%async_computation.1 | async-start | bytes 6684672 | tf_op jit(solution)/shard_map/all_gather | solution.py:111
  17.5 229.6 %all-gather.9.cloned.1.call-start = ((), (), s32[]{:S(2)}) async-start(), calls=%async_computation.2 | async-start | bytes 6684672 | tf_op jit(solution)/shard_map/all_gather | solution.py:110
  18.5 304.1 %all-gather.11.cloned.1.call-start = ((), (), s32[]{:S(2)}) async-start(), calls=%async_computation.3 | async-start | bytes 6684672 | tf_op jit(solution)/shard_map/all_gather | solution.py:112
  334.2 8.4 %copy-start = (f32[12,128]{1,0:T(8,128)S(1)}, f32[12,128]{1,0:T(8,128)}, u32[]{:S(2)}) copy-start(f32[12,128]{1,0:T(8,128)} %get-tuple-element.331) | copy-start | bytes 18436 | tf_op jit(solution)/shard_map/while
  342.6 0.6 copy-start.1
  346.1 9.1 %copy-start = (f32[12,128]{1,0:T(8,128)S(1)}, f32[12,128]{1,0:T(8,128)}, u32[]{:S(2)}) copy-start(f32[12,128]{1,0:T(8,128)} %get-tuple-element.331) | copy-start | bytes 18436 | tf_op jit(solution)/shard_map/while
  355.2 0.6 copy-start.1
  358.6 9.1 %copy-start = (f32[12,128]{1,0:T(8,128)S(1)}, f32[12,128]{1,0:T(8,128)}, u32[]{:S(2)}) copy-start(f32[12,128]{1,0:T(8,128)} %get-tuple-element.331) | copy-start | bytes 18436 | tf_op jit(solution)/shard_map/while
  367.8 0.6 copy-start.1
  371.2 9.1 %copy-start = (f32[12,128]{1,0:T(8,128)S(1)}, f32[12,128]{1,0:T(8,128)}, u32[]{:S(2)}) copy-start(f32[12,128]{1,0:T(8,128)} %get-tuple-element.331) | copy-start | bytes 18436 | tf_op jit(solution)/shard_map/while
  380.3 0.6 copy-start.1
  383.8 9.1 %copy-start = (f32[12,128]{1,0:T(8,128)S(1)}, f32[12,128]{1,0:T(8,128)}, u32[]{:S(2)}) copy-start(f32[12,128]{1,0:T(8,128)} %get-tuple-element.331) | copy-start | bytes 18436 | tf_op jit(solution)/shard_map/while
  392.9 0.6 copy-start.1
  396.4 9.1 %copy-start = (f32[12,128]{1,0:T(8,128)S(1)}, f32[12,128]{1,0:T(8,128)}, u32[]{:S(2)}) copy-start(f32[12,128]{1,0:T(8,128)} %get-tuple-element.331) | copy-start | bytes 18436 | tf_op jit(solution)/shard_map/while
  405.5 0.6 copy-start.1
  408.9 9.1 %copy-start = (f32[12,128]{1,0:T(8,128)S(1)}, f32[12,128]{1,0:T(8,128)}, u32[]{:S(2)}) copy-start(f32[12,128]{1,0:T(8,128)} %get-tuple-element.331) | copy-start | bytes 18436 | tf_op jit(solution)/shard_map/while
  418.1 0.6 copy-start.1
  421.5 9.1 %copy-start = (f32[12,128]{1,0:T(8,128)S(1)}, f32[12,128]{1,0:T(8,128)}, u32[]{:S(2)}) copy-start(f32[12,128]{1,0:T(8,128)} %get-tuple-element.331) | copy-start | bytes 18436 | tf_op jit(solution)/shard_map/while
  430.6 0.6 copy-start.1
  434.1 9.1 %copy-start = (f32[12,128]{1,0:T(8,128)S(1)}, f32[12,128]{1,0:T(8,128)}, u32[]{:S(2)}) copy-start(f32[12,128]{1,0:T(8,128)} %get-tuple-element.331) | copy-start | bytes 18436 | tf_op jit(solution)/shard_map/while
  443.2 0.6 copy-start.1
  446.7 9.1 %copy-start = (f32[12,128]{1,0:T(8,128)S(1)}, f32[12,128]{1,0:T(8,128)}, u32[]{:S(2)}) copy-start(f32[12,128]{1,0:T(8,128)} %get-tuple-element.331) | copy-start | bytes 18436 | tf_op jit(solution)/shard_map/while
  455.8 0.6 copy-start.1
  459.2 9.1 %copy-start = (f32[12,128]{1,0:T(8,128)S(1)}, f32[12,128]{1,0:T(8,128)}, u32[]{:S(2)}) copy-start(f32[12,128]{1,0:T(8,128)} %get-tuple-element.331) | copy-start | bytes 18436 | tf_op jit(solution)/shard_map/while
  468.4 0.6 copy-start.1
  471.8 9.1 %copy-start = (f32[12,128]{1,0:T(8,128)S(1)}, f32[12,128]{1,0:T(8,128)}, u32[]{:S(2)}) copy-start(f32[12,128]{1,0:T(8,128)} %get-tuple-element.331) | copy-start | bytes 18436 | tf_op jit(solution)/shard_map/while
  480.9 0.6 copy-start.1
  484.4 9.1 %copy-start = (f32[12,128]{1,0:T(8,128)S(1)}, f32[12,128]{1,0:T(8,128)}, u32[]{:S(2)}) copy-start(f32[12,128]{1,0:T(8,128)} %get-tuple-element.331) | copy-start | bytes 18436 | tf_op jit(solution)/shard_map/while
  493.5 0.6 copy-start.1
  496.9 9.1 %copy-start = (f32[12,128]{1,0:T(8,128)S(1)}, f32[12,128]{1,0:T(8,128)}, u32[]{:S(2)}) copy-start(f32[12,128]{1,0:T(8,128)} %get-tuple-element.331) | copy-start | bytes 18436 | tf_op jit(solution)/shard_map/while
  506.1 0.6 copy-start.1
  509.5 9.1 %copy-start = (f32[12,128]{1,0:T(8,128)S(1)}, f32[12,128]{1,0:T(8,128)}, u32[]{:S(2)}) copy-start(f32[12,128]{1,0:T(8,128)} %get-tuple-element.331) | copy-start | bytes 18436 | tf_op jit(solution)/shard_map/while
  518.6 0.6 copy-start.1
  522.1 9.1 %copy-start = (f32[12,128]{1,0:T(8,128)S(1)}, f32[12,128]{1,0:T(8,128)}, u32[]{:S(2)}) copy-start(f32[12,128]{1,0:T(8,128)} %get-tuple-element.331) | copy-start | bytes 18436 | tf_op jit(solution)/shard_map/while
  531.2 0.6 copy-start.1
  531.8 2.5 copy-start.3
Sparse Core Ops, SparseCore 0:
  16.7 78.7 all-gather.4
  98.1 73.1 all-gather.6
  173.9 73.1 all-gather.8
  249.5 73.1 all-gather.10
where the time goes:
time: 630 us; the launch traced here: 623 us
  waiting for transfers between devices  240 us (38%)
  matrix products  150 us (24%)
  blocking collectives  102 us (16%)
  local copies, waits for them, and re-layouts  74 us (12%)
  other arithmetic  41 us (7%)
  between operations  14.6 us (2%)
    psum x1, blocking collectives, local(): summed = lax.psum(partial_grad, ('ctx', 'dp'))  75.7 us
    all_gather x1, waiting for transfers between devices, local(): value_part = lax.all_gather(value_heads, 'ctx', axis=1, tiled=True)  67.1 us
    all_gather x1, waiting for transfers between devices, local(): tvalue_part = lax.all_gather(tvalue_heads, 'ctx', axis=1, tiled=True)  67 us
    all_gather x1, waiting for transfers between devices, local(): tkey_part = lax.all_gather(tkey_rot, 'ctx', axis=1, tiled=True)  58.9 us
    all_gather x1, waiting for transfers between devices, local(): key_part = lax.all_gather(key_rot, 'ctx', axis=1, tiled=True)  46.9 us
    all_gather x1, blocking collectives, local(): all_ids = lax.all_gather(clip_ids, 'ctx', axis=1, tiled=True)[0]  25.8 us
    dot_general x16, matrix products, attend(): jnp.einsum('hqk,hkd->hqd', weights_b, value_blk, preferred_element_type=j...  25.1 us
    dot_general x16, matrix products, attend(): jnp.einsum('hqk,hkd->hqd', tilted_b, value_blk, preferred_element_type=jn...  24.9 us
  transfers between devices with their start and end apart: 4, of which 4 were waited for; matrix products, arithmetic and copies ran while one was open for 6% of the time, Pallas kernels for 0%

commit v1 on v0

--- a/solution.py
+++ b/solution.py
@@ -134,7 +134,8 @@
     projected = jnp.dot(tangent_rows, out_weight, preferred_element_type=jnp.float32)
     branch = (layer_scale * projected).astype(jnp.bfloat16)[None]
     partial_grad = jnp.sum(cotangent[0].astype(jnp.float32) * projected, axis=0)
-    summed = lax.psum(partial_grad, ("ctx", "dp"))
+    parts = lax.all_gather(partial_grad, ("ctx", "dp"))
+    summed = jnp.sum(parts, axis=0)
     count_all = lax.axis_size("ctx") * lax.axis_size("dp") * tok_rows
     return (branch, summed / math.sqrt(count_all))
 

time: 630 us -> 1260 us (2.00)
  waiting for transfers between devices: 240 us -> 942 us
  blocking collectives: 102 us -> 26.4 us
    all_gather x0 -> x1, waiting for transfers between devices: none -> 702 us  [local(): parts = lax.all_gather(partial_grad, ('ctx', 'dp'))]
    psum x1 -> x0, blocking collectives: 75.7 us -> none  [local(): summed = lax.psum(partial_grad, ('ctx', 'dp'))]
  transfers between devices with their start and end apart: 4 -> 5, of which waited for: 4 -> 5; matrix products, arithmetic and copies ran while one was open for 6% -> 3% of each run, Pallas kernels for 0% -> 0%
where the time goes in v1:
time: 1260 us; the launch traced here: 1250 us
  waiting for transfers between devices  942 us (75%)
  matrix products  151 us (12%)
  local copies, waits for them, and re-layouts  77 us (6%)
  other arithmetic  41.2 us (3%)
  blocking collectives  26.4 us (2%)
  between operations  14.6 us (1%)
    all_gather x1, waiting for transfers between devices, local(): parts = lax.all_gather(partial_grad, ('ctx', 'dp'))  702 us
    all_gather x1, waiting for transfers between devices, local(): value_part = lax.all_gather(value_heads, 'ctx', axis=1, tiled=True)  67.1 us
    all_gather x1, waiting for transfers between devices, local(): tvalue_part = lax.all_gather(tvalue_heads, 'ctx', axis=1, tiled=True)  67 us
    all_gather x1, waiting for transfers between devices, local(): tkey_part = lax.all_gather(tkey_rot, 'ctx', axis=1, tiled=True)  59 us
    all_gather x1, waiting for transfers between devices, local(): key_part = lax.all_gather(key_rot, 'ctx', axis=1, tiled=True)  46.2 us
    all_gather x1, blocking collectives, local(): all_ids = lax.all_gather(clip_ids, 'ctx', axis=1, tiled=True)[0]  26.4 us
  transfers between devices with their start and end apart: 5, of which 5 were waited for; matrix products, arithmetic and copies ran while one was open for 3% of the time, Pallas kernels for 0%

profile of v1, /device:TPU:1, one launch (start us, length us, event | category | flops | bytes accessed | tf_op | source)
XLA Modules:
  0.0 1254.0 jit_solution(17240583803942315129)
XLA Ops:
  18.6 1.9 copy.70
  22.9 26.4 %all_gather.21 = s32[1,2048]{1,0:T(1,128)} all-gather(s32[1,128]{1,0:T(1,128)} %param.19), channel_id=1, replica_groups=mesh['ctx'=16,'dp'=16] {'ctx'}, dimensions={1}, use_global_device_ids=true | all-gather | bytes 8704 | tf_op jit(solution)/shard_map/all_gather | solution.py:105
  49.4 46.2 %all-gather.7.cloned.1.call-done = bf16[12,2048,128]{1,2,0:T(8,128)(2,1)} async-done(((bf16[12,128,128]{1,2,0:T(8,128)(2,1)}), bf16[12,2048,128]{1,2,0:T(8,128)(2,1)}) %all-gather.7.cloned.1.call-update) | async-done | bytes 6291472 | tf_op jit(solution)/shard_map/all_gather | solution.py:109
  95.6 7.8 copy.86
  103.3 9.0 copy.63
  112.3 59.0 %all-gather.9.cloned.1.call-done = bf16[12,2048,128]{1,2,0:T(8,128)(2,1)} async-done(((bf16[12,128,128]{1,2,0:T(8,128)(2,1)}), bf16[12,2048,128]{1,2,0:T(8,128)(2,1)}) %all-gather.9.cloned.1.call-update) | async-done | bytes 6291472 | tf_op jit(solution)/shard_map/all_gather | solution.py:111
  171.3 8.7 copy.67
  180.0 67.1 %all-gather.11.cloned.1.call-done = bf16[12,2048,128]{1,2,0:T(8,128)(2,1)} async-done(((bf16[12,128,128]{1,2,0:T(8,128)(2,1)}), bf16[12,2048,128]{1,2,0:T(8,128)(2,1)}) %all-gather.11.cloned.1.call-update) | async-done | bytes 6291472 | tf_op jit(solution)/shard_map/all_gather | solution.py:110
  247.1 8.6 copy.69
  255.7 67.0 %all-gather.13.cloned.1.call-done = bf16[12,2048,128]{1,2,0:T(8,128)(2,1)} async-done(((bf16[12,128,128]{1,2,0:T(8,128)(2,1)}), bf16[12,2048,128]{1,2,0:T(8,128)(2,1)}) %all-gather.13.cloned.1.call-update) | async-done | bytes 6291472 | tf_op jit(solution)/shard_map/all_gather | solution.py:112
  322.7 8.7 copy.71
  331.4 200.7 %while.21 = (s32[]{:T(128)}, f32[12,128]{1,0:T(8,128)S(1)}, f32[12,128]{1,0:T(8,128)}, f32[12,128]{1,0:T(8,128)}, f32[12,128,128]{2,1,0:T(8,128)S(1)}, /*index=5...) while((s32[]{:T(128)}, f32[12,128]{1,0:T(8,128)S(1)}, ...), condition=%wide.region_4.5_spmd.clone, body=%wide.region_0.4_spmd.clone.sunk | while | flops 306735616 | bytes 14789864 | solution.py:127
  337.8 1.6 convolution_add_fusion.9
  339.4 1.6 convolution_add_fusion.8
  340.9 1.6 convolution_add_fusion.7
  346.1 1.5 fusion.72
  350.4 1.6 convolution_add_fusion.9
  351.9 1.6 convolution_add_fusion.8
  353.5 1.6 convolution_add_fusion.7
  363.0 1.6 convolution_add_fusion.9
  364.5 1.6 convolution_add_fusion.8
  366.1 1.6 convolution_add_fusion.7
  375.6 1.6 convolution_add_fusion.9
  377.1 1.6 convolution_add_fusion.8
  378.7 1.6 convolution_add_fusion.7
  388.1 1.6 convolution_add_fusion.9
  389.7 1.6 convolution_add_fusion.8
  391.3 1.6 convolution_add_fusion.7
  400.7 1.6 convolution_add_fusion.9
  402.3 1.6 convolution_add_fusion.8
  403.8 1.6 convolution_add_fusion.7
  413.3 1.6 convolution_add_fusion.9
  414.9 1.6 convolution_add_fusion.8
  416.4 1.6 convolution_add_fusion.7
  425.9 1.6 convolution_add_fusion.9
  427.4 1.6 convolution_add_fusion.8
  429.0 1.6 convolution_add_fusion.7
  438.5 1.6 convolution_add_fusion.9
  440.0 1.6 convolution_add_fusion.8
  441.6 1.6 convolution_add_fusion.7
  451.1 1.6 convolution_add_fusion.9
  452.6 1.6 convolution_add_fusion.8
  454.2 1.6 convolution_add_fusion.7
  463.6 1.6 convolution_add_fusion.9
  465.2 1.6 convolution_add_fusion.8
  466.8 1.6 convolution_add_fusion.7
  476.2 1.6 convolution_add_fusion.9
  477.8 1.6 convolution_add_fusion.8
  479.3 1.6 convolution_add_fusion.7
  488.8 1.6 convolution_add_fusion.9
  490.4 1.6 convolution_add_fusion.8
  491.9 1.6 convolution_add_fusion.7
  501.4 1.6 convolution_add_fusion.9
  503.0 1.6 convolution_add_fusion.8
  504.5 1.6 convolution_add_fusion.7
  514.0 1.6 convolution_add_fusion.9
  515.5 1.6 convolution_add_fusion.8
  517.1 1.6 convolution_add_fusion.7
  526.6 1.6 convolution_add_fusion.9
  528.1 1.6 convolution_add_fusion.8
  529.7 1.6 convolution_add_fusion.7
  534.5 7.0 fusion.32
  541.5 702.4 %all-gather.15.cloned.1.call-done = f32[786432]{0:T(1024)} async-done(((f32[3072]{0:T(1024)}), f32[786432]{0:T(1024)}) %all-gather.15.cloned.1.call-update) | async-done | bytes 3145744 | tf_op jit(solution)/shard_map/all_gather | solution.py:137
  1243.9 2.8 reshape.134
  (269 shorter events, 138.7 us)
Async XLA Ops:
  7.2 88.4 %all-gather.7.cloned.1.call-start = ((), (), s32[]{:S(2)}) async-start(), calls=%async_computation | async-start | bytes 6684672 | tf_op jit(solution)/shard_map/all_gather | solution.py:109
  11.7 5.9 copy-start.2
  16.6 154.7 %all-gather.9.cloned.1.call-start = ((), (), s32[]{:S(2)}) async-start(), calls=%async_computation.1 | async-start | bytes 6684672 | tf_op jit(solution)/shard_map/all_gather | solution.py:111
  17.5 229.5 %all-gather.11.cloned.1.call-start = ((), (), s32[]{:S(2)}) async-start(), calls=%async_computation.2 | async-start | bytes 6684672 | tf_op jit(solution)/shard_map/all_gather | solution.py:110
  18.5 304.1 %all-gather.13.cloned.1.call-start = ((), (), s32[]{:S(2)}) async-start(), calls=%async_computation.3 | async-start | bytes 6684672 | tf_op jit(solution)/shard_map/all_gather | solution.py:112
  20.5 1223.3 %all-gather.15.cloned.1.call-start = ((), (), s32[]{:S(2)}) async-start(), calls=%async_computation.4 | async-start | bytes 3158016 | tf_op jit(solution)/shard_map/all_gather | solution.py:137
  334.2 8.4 copy-start
  342.7 0.6 copy-start.1
  346.1 9.1 copy-start
  355.2 0.6 copy-start.1
  358.7 9.1 copy-start
  367.8 0.6 copy-start.1
  371.3 9.1 copy-start
  380.4 0.6 copy-start.1
  383.9 9.1 copy-start
  393.0 0.6 copy-start.1
  396.4 9.1 copy-start
  405.6 0.6 copy-start.1
  409.0 9.1 copy-start
  418.2 0.6 copy-start.1
  421.6 9.1 copy-start
  430.7 0.6 copy-start.1
  434.2 9.1 copy-start
  443.3 0.6 copy-start.1
  446.8 9.1 copy-start
  455.9 0.6 copy-start.1
  459.4 9.1 copy-start
  468.5 0.6 copy-start.1
  472.0 9.1 copy-start
  481.1 0.6 copy-start.1
  484.5 9.1 copy-start
  493.7 0.6 copy-start.1
  497.1 9.1 copy-start
  506.3 0.6 copy-start.1
  509.7 9.1 copy-start
  518.8 0.6 copy-start.1
  522.3 9.1 copy-start
  531.4 0.6 copy-start.1
  532.0 2.5 copy-start.3
Sparse Core Ops, SparseCore 0:
  16.7 78.7 all-gather.6
  98.1 73.1 all-gather.8
  173.9 73.1 all-gather.10
  249.5 73.1 all-gather.12
  541.6 702.1 all-gather.14
